TPU v7x, 32 devices: a whole 2x2x4 slice. The times are simulated.
32 devices in a mesh: groups: 2 (over y), seq: 4 (over z), mp: 2 (over x), rep: 2 (over core).
Axes of the slice: x: 2, y: 2, z: 4, core: 2. Of those that a mesh axis runs over, the one named last changes fastest.
Arguments:
- tokens: bfloat16 [8192, 2240], P(('groups', 'seq', 'rep')), parts along dimension 0, may hold values from -8 to 8
- slot_image: int32 [32], P(('groups', 'seq', 'rep')), parts along dimension 0, may hold values from 0 to 5, as said below
- modulation: float32 [12, 3, 2240], P('groups'), parts along dimension 0, may hold values from -3 to 3
- w_qkv: bfloat16 [2240, 3, 1280], P('rep', None, 'mp'), may hold values from -0.125 to 0.125
- w_out: bfloat16 [1280, 2240], P('rep', 'mp'), may hold values from -0.15625 to 0.15625
Outputs:
- updated: bfloat16 [8192, 2240], P(('groups', 'seq', 'rep'), 'mp'), parts along dimension 0
There are 2 independent parts, one for each index of `groups`. A program takes and returns all parts, laid end to end along the dimension named above; an argument that names none is the same for every part. Nothing has to cross between parts.
Inputs may be any that keep to these rules, and one draw needn't show every extreme that they name: `slot_image`: every one of the 6 images owns one tile slot or more.
All inputs are finite; a program needn't handle non-finite values.
Results may differ from a plain program's by a relative error of at most 0.0036.
Values may be sent and summed in bfloat16 or wider, within the bound.
No kernel may reach another device: no remote copies, remote signals or barrier semaphores. Data moves between devices by JAX's collectives and lax.ppermute only.
A program may use at most 128 MiB of HBM per device.

v0:
```python
import jax
import jax.numpy as jnp
from jax import lax
from jax.sharding import PartitionSpec as P

D = 2240
HD = 32


def body(tokens, slot_image, modulation, w_qkv, w_out):
    hi = lax.Precision.HIGHEST
    tiles = slot_image.shape[0]
    rows = tokens.shape[0]
    tile_len = rows // tiles
    images = modulation.shape[0]
    width = w_qkv.shape[2]
    per_dev = width // HD
    picker = (slot_image[:, None] == jnp.arange(images, dtype=jnp.int32)[None, :]).astype(
        jnp.float32
    )
    per_tile = jnp.dot(picker, modulation.reshape(images, 3 * D), precision=hi).reshape(tiles, 3, D)
    xf = tokens.astype(jnp.float32).reshape(tiles, tile_len, D)
    mean = jnp.mean(xf, axis=2, keepdims=True)
    var = jnp.mean((xf - mean) ** 2, axis=2, keepdims=True)
    normed = (xf - mean) / jnp.sqrt(var + 1e-06)
    modulated = (normed * (1.0 + per_tile[:, None, 1, :]) + per_tile[:, None, 0, :]).astype(
        jnp.bfloat16
    )
    modulated = modulated.reshape(rows, D)
    qkv = jnp.einsum(
        "td,dcm->tcm",
        modulated,
        lax.all_gather(w_qkv, "rep", axis=0, tiled=True),
        preferred_element_type=jnp.float32,
    )
    qkv = qkv.reshape(tiles, tile_len, 3, per_dev, HD)
    query = jax.nn.relu(qkv[:, :, 0]).astype(jnp.bfloat16)
    keyf = jax.nn.relu(qkv[:, :, 1]).astype(jnp.bfloat16)
    value = qkv[:, :, 2].astype(jnp.bfloat16)
    tile_state = jnp.einsum("slhe,slhf->shef", keyf, value, preferred_element_type=jnp.float32)
    tile_ksum = jnp.sum(keyf.astype(jnp.float32), axis=1)
    state = jnp.einsum("si,shef->ihef", picker, tile_state, precision=hi)
    ksum = jnp.einsum("si,she->ihe", picker, tile_ksum, precision=hi)
    state, ksum = lax.psum((state, ksum), ("seq", "rep"))
    own_state = jnp.einsum("si,ihef->shef", picker, state, precision=hi)
    own_ksum = jnp.einsum("si,ihe->she", picker, ksum, precision=hi)
    query_wide = query.astype(jnp.float32)
    numer = jnp.einsum("slhe,shef->slhf", query_wide, own_state, precision=hi)
    denom = jnp.einsum("slhe,she->slh", query_wide, own_ksum, precision=hi) + 1e-06
    attn = (numer / denom[..., None]).astype(jnp.bfloat16).reshape(rows, per_dev * HD)
    out_full = lax.all_gather(w_out, "rep", axis=0, tiled=True)
    cols = out_full.shape[1]
    projected = jnp.dot(
        lax.all_gather(attn, "mp", axis=1, tiled=True), out_full, preferred_element_type=jnp.float32
    )
    offset = lax.axis_index("mp") * cols
    own_tokens = (
        lax.dynamic_slice_in_dim(tokens, offset, cols, 1)
        .astype(jnp.float32)
        .reshape(tiles, tile_len, cols)
    )
    gate = lax.dynamic_slice_in_dim(per_tile[:, 2, :], offset, cols, 1)
    updated = own_tokens + gate[:, None, :] * projected.reshape(tiles, tile_len, cols)
    return updated.astype(jnp.bfloat16).reshape(rows, cols)


def solution(mesh):
    return jax.shard_map(
        body,
        mesh=mesh,
        in_specs=(
            P(("groups", "seq", "rep"), None),
            P(("groups", "seq", "rep")),
            P("groups", None, None),
            P("rep", None, "mp"),
            P("rep", "mp"),
        ),
        out_specs=P(("groups", "seq", "rep"), "mp"),
        check_vma=False,
    )
```

profile of v0, /device:TPU:0, one launch (start us, length us, event | category | flops | bytes accessed | tf_op | source)
XLA Modules:
  0.0 175.1 jit_solution(10275999285317942195)
XLA Ops:
  6.5 0.0 copy-start.1
  6.5 0.0 all-gather.4.cloned.1.call-start
  6.5 0.0 copy-start.3
  6.5 0.7 all-gather.4.cloned.1.call-update
  7.3 0.0 all-reduce.2.cloned.1.call-start
  7.3 0.2 copy-done.1
  7.5 0.2 reshape.54
  7.7 0.1 dot_general.41
  7.8 0.0 copy-done.3
  7.8 0.3 fusion.24
  8.1 0.4 copy.12
  8.5 2.7 %mul.34 = f32[2,256,2240]{1,0,2:T(2,128)S(1)} broadcast(f32[2,2240]{0,1:T(8,128)S(1)} %copy.12), dimensions={0,2} | broadcast | bytes 4605440 | tf_op jit(solution)/shard_map/mul | solution.py:26
  11.3 2.6 %copy.34 = f32[280,8,2,256]{3,1,2,0:T(8,128)} copy(f32[280,8,2,256]{3,2,1,0:T(2,128)S(1)} %bitcast.80) | data formatting | bytes 9175040
  13.8 0.4 copy.13
  14.2 0.0 slice-start
  14.2 2.7 %add.57 = f32[2,256,2240]{1,0,2:T(2,128)S(1)} broadcast(f32[2,2240]{0,1:T(8,128)S(1)} %copy.13), dimensions={0,2} | broadcast | bytes 4605440 | tf_op jit(solution)/shard_map/add | solution.py:26
  17.0 0.0 copy-start
  17.0 0.0 slice-start.1
  17.0 0.5 copy.35
  17.5 1.5 copy-done
  19.0 0.4 convert_reduce_fusion
  19.4 0.7 fusion.2
  20.1 0.0 slice-done
  20.1 0.0 slice-done.1
  20.1 3.0 %fusion.5 = bf16[512,2240]{0,1:T(8,128)(2,1)} fusion(f32[512,2240]{0,1:T(8,128)S(1)} %bitcast.79, f32[512,2240]{0,1:T(8,128)S(1)} %bitcast.78, bf16[512,2240]{0,1:T(8,128)(2,1)S(1)} %copy-done, f32[512]{0:T(512)S(1)} %add_sqrt_fusion, f32[512]{0:T(512)S(1)} %broadcast_multiply_fusion), kind=kLoop, calls=%fused_computation.7 | loop fusion | flops 6881280 | bytes 13766656 | tf_op jit(solution)/shard_map/convert_element_type | solution.py:26
  23.1 6.1 %dot_general.43 = bf16[2,256,2240]{1,0,2:T(2,128)(2,1)} reshape(bf16[512,2240]{0,1:T(8,128)(2,1)} %fusion.5) | data formatting | bytes 4587520 | tf_op jit(solution)/shard_map/td,dcm->tcm/dot_general | solution.py:30
  29.2 1.7 all-gather.4.cloned.1.call-done
  30.9 13.2 %copy.14 = bf16[3,640,2240]{2,1,0:T(8,128)(2,1)} copy(bf16[3,640,2240]{1,2,0:T(8,128)(2,1)} %bitcast.84) | data formatting | bytes 17203200 | tf_op jit(solution)/shard_map/td,dcm->tcm/dot_general | solution.py:30
  44.1 8.9 %fusion.10 = bf16[2,256,3,20,32]{1,4,3,2,0:T(8,128)(2,1)S(1)} fusion(bf16[3,20,32,2240,1]{3,2,1,0,4:T(8,128)(2,1)} %bitcast.83, bf16[2,256,2240,1,1]{1,0,2,4,3:T(2,128)(2,1)} %bitcast.88), kind=kOutput, calls=%fused_computation.13 | convolution fusion | flops 4404019200 | bytes 12861440 | tf_op jit(solution)/shard_map/td,dcm->tcm/dot_general | solution.py:30
  53.1 0.0 copy-start.2
  53.1 0.3 fusion.18
  53.4 1.9 %fusion.22 = f32[6,20,32,32]{3,0,2,1:T(8,128)S(1)} fusion(f32[2,20,32,32]{3,2,1,0:T(8,128)S(1)} %fusion.18, s32[2]{0:T(128)S(1)} %copy-done.3), kind=kOutput, calls=%fused_computation.30 | convolution fusion | flops 2949132 | bytes 655368 | tf_op jit(solution)/shard_map/si,shef->ihef/dot_general | solution.py:42
  55.4 0.0 copy-done.2
  55.4 1.7 copy.20
  57.1 0.0 all-reduce.2.cloned.1.call-update
  57.1 0.0 all-gather.8.cloned.1.call-start
  57.2 0.7 all-gather.8.cloned.1.call-update
  57.8 0.0 all-gather.6.cloned.1.call-start
  57.9 1.3 convert_reduce_fusion.1
  59.2 0.3 fusion.33
  59.6 31.6 %psum.15 = f32[6,20,32]{2,1,0:T(8,128)S(1)} all-reduce(f32[6,20,32]{2,1,0:T(8,128)S(1)} %copy.24), channel_id=1, replica_groups=mesh['groups'=2,'seq'=4,'mp'=2,'rep'=2] {'seq','rep'}, use_global_device_ids=true, to_apply=%region_4.5 | all-reduce | flops 3840 | bytes 30720 | tf_op jit(solution)/shard_map/psum | solution.py:44
  91.2 0.2 convolution_bitcast_fusion.1
  91.4 1.5 fusion.27
  92.9 30.4 %all-reduce.2.cloned.1.call-done = f32[6,20,32,32]{3,2,1,0:T(8,128)} async-done(((f32[6,20,32,32]{3,2,1,0:T(8,128)}), f32[6,20,32,32]{3,2,1,0:T(8,128)}) %all-reduce.2.cloned.1.call-update) | async-done | bytes 491536 | tf_op jit(solution)/shard_map/psum | solution.py:44
  123.3 3.9 %fusion.8 = f32[2,20,32,32]{3,0,2,1:T(2,128)S(1)} fusion(f32[6,20,32,32]{3,2,1,0:T(8,128)} %all-reduce.2.cloned.1.call-done, s32[2]{0:T(128)S(1)} %copy-done.3), kind=kOutput, calls=%fused_computation.11 | convolution fusion | flops 2949132 | bytes 655368 | tf_op jit(solution)/shard_map/si,ihef->shef/dot_general | solution.py:45
  127.2 1.9 %fusion.13 = bf16[2,256,20,32]{1,3,2,0:T(8,128)(2,1)S(1)} fusion(f32[2,20,32,32]{3,0,2,1:T(2,128)S(1)} %fusion.8, f32[2,256,20]{1,2,0:T(8,128)S(1)} %fusion.31, bf16[2,256,3,20,32]{1,4,3,2,0:T(8,128)(2,1)} %copy-done.2), kind=kOutput, calls=%fused_computation.17 | convolution fusion | flops 127467520 | bytes 1515520 | tf_op jit(solution)/shard_map/slhe,shef->slhf/dot_general | solution.py:48
  129.1 0.7 copy.16
  129.8 0.9 copy.36
  130.7 0.0 all-gather.6.cloned.1.call-update
  130.8 0.1 dynamic-slice_bitcast_fusion
  130.8 0.2 copy.11
  131.1 1.3 mul.31
  132.5 1.6 copy.33
  134.1 2.0 %all-gather.8.cloned.1.call-done = bf16[1280,1120]{0,1:T(8,128)(2,1)} async-done(((bf16[640,1120]{0,1:T(8,128)(2,1)}), bf16[1280,1120]{0,1:T(8,128)(2,1)}) %all-gather.8.cloned.1.call-update) | async-done | bytes 2867216 | tf_op jit(solution)/shard_map/all_gather | solution.py:51
  136.1 26.8 %all-gather.6.cloned.1.call-done = bf16[512,1280]{0,1:T(8,128)(2,1)} async-done(((bf16[512,640]{0,1:T(8,128)(2,1)}), bf16[512,1280]{0,1:T(8,128)(2,1)}) %all-gather.6.cloned.1.call-update) | async-done | bytes 1310736 | tf_op jit(solution)/shard_map/all_gather | solution.py:54
  162.9 5.6 %fusion.7 = bf16[512,1120]{0,1:T(8,128)(2,1)} fusion(f32[512,1120]{0,1:T(8,128)} %bitcast.87, bf16[1280,1120]{0,1:T(8,128)(2,1)} %all-gather.8.cloned.1.call-done, bf16[512,1280]{0,1:T(8,128)(2,1)} %all-gather.6.cloned.1.call-done, bf16[512,2240]{0,1:T(8,128)(2,1)S(1)} %copy-done, s32[]{:T(128)S(6)} %select_n.4), kind=kOutput, calls=%fused_computation.10 | convolution fusion | flops 1470300160 | bytes 8765444 | tf_op jit(solution)/shard_map/dot_general | solution.py:53
  (6 shorter events, 0.1 us)
Async XLA Ops:
  6.5 0.9 copy-start.1
  6.5 24.4 %all-gather.4.cloned.1.call-start = ((), (), s32[]{:S(2)}) async-start(), calls=%async_computation | async-start | bytes 12902400 | tf_op jit(solution)/shard_map/all_gather | solution.py:33
  6.5 1.3 copy-start.3
  7.3 116.1 %all-reduce.2.cloned.1.call-start = ((), (), s32[]{:S(2)}) async-start(), calls=%async_computation.1 | async-start | bytes 3932160 | tf_op jit(solution)/shard_map/psum | solution.py:44
  14.2 5.9 %slice-start = ((s8[4587520]{0:T(1024)(128)(4,1)}), s8[4194304]{0:T(1024)(128)(4,1)S(1)}, s32[]{:S(2)}) async-start(s8[4587520]{0:T(1024)(128)(4,1)} %bitcast.76), calls=%async_computation.4 | async-start | bytes 8388608
  17.0 2.1 %copy-start = (bf16[512,2240]{0,1:T(8,128)(2,1)S(1)}, bf16[512,2240]{0,1:T(8,128)(2,1)}, u32[]{:S(2)}) copy-start(bf16[512,2240]{0,1:T(8,128)(2,1)} %param.5) | copy-start | bytes 6881284
  17.0 3.1 %slice-start.1 = ((s8[4587520]{0:T(1024)(128)(4,1)}), s8[393216]{0:T(1024)(128)(4,1)S(1)}, s32[]{:S(2)}) async-start(s8[4587520]{0:T(1024)(128)(4,1)} %bitcast.76), calls=%async_computation.5 | async-start | bytes 786432
  53.1 2.3 %copy-start.2 = (bf16[2,256,3,20,32]{1,4,3,2,0:T(8,128)(2,1)}, bf16[2,256,3,20,32]{1,4,3,2,0:T(8,128)(2,1)S(1)}, u32[]{:S(2)}) copy-start(bf16[2,256,3,20,32]{1,4,3,2,0:T(8,128)(2,1)S(1)} %fusion.10) | copy-start | bytes 5898244
  57.1 79.0 %all-gather.8.cloned.1.call-start = ((), (), s32[]{:S(2)}) async-start(), calls=%async_computation.3 | async-start | bytes 4300800 | tf_op jit(solution)/shard_map/all_gather | solution.py:51
  57.8 105.1 %all-gather.6.cloned.1.call-start = ((), (), s32[]{:S(2)}) async-start(), calls=%async_computation.2 | async-start | bytes 1966080 | tf_op jit(solution)/shard_map/all_gather | solution.py:54
Sparse Core Ops, SparseCore 0:
  8.9 21.9 all-gather.3
  57.2 66.0 all-reduce.1
  124.9 11.1 all-gather.7
  137.5 25.3 all-gather.5
where the time goes:
time: 176 us; the launch traced here: 175 us
  waiting for transfers between devices  62.4 us (35%)
  local copies, waits for them, and re-layouts  37.3 us (21%)
  blocking collectives  31.6 us (18%)
  matrix products  24.9 us (14%)
  between operations  13.3 us (8%)
  other arithmetic  5.39 us (3%)
    psum x1, blocking collectives, body(): state, ksum = lax.psum((state, ksum), ('seq', 'rep'))  31.6 us
    psum x1, waiting for transfers between devices, body(): state, ksum = lax.psum((state, ksum), ('seq', 'rep'))  30.4 us
    all_gather x1, waiting for transfers between devices, body(): lax.all_gather(attn, 'mp', axis=1, tiled=True)  26.8 us
    dot_general x2, local copies, waits for them, and re-layouts, body(): jnp.einsum('td,dcm->tcm', modulated, lax.all_gather(w_qkv, 'rep', axis=0,...  19.3 us
    dot_general x1, matrix products, body(): jnp.einsum('td,dcm->tcm', modulated, lax.all_gather(w_qkv, 'rep', axis=0,...  8.95 us
    unnamed x16, local copies, waits for them, and re-layouts  7.35 us
    dot_general x1, matrix products, body(): jnp.dot(lax.all_gather(attn, 'mp', axis=1, tiled=True), out_full, preferr...  5.59 us
    dot_general x1, matrix products, body(): own_state = jnp.einsum('si,ihef->shef', picker, state, precision=hi)  3.93 us
  transfers between devices with their start and end apart: 4, of which 4 were waited for; matrix products, arithmetic and copies ran while one was open for 19% of the time, Pallas kernels for 0%

commit v1 on v0

--- a/solution.py
+++ b/solution.py
@@ -41,7 +41,7 @@
     tile_ksum = jnp.sum(keyf.astype(jnp.float32), axis=1)
     state = jnp.einsum("si,shef->ihef", picker, tile_state, precision=hi)
     ksum = jnp.einsum("si,she->ihe", picker, tile_ksum, precision=hi)
-    state, ksum = lax.psum((state, ksum), ("seq", "rep"))
+    state, ksum = lax.psum(lax.psum((state, ksum), "rep"), "seq")
     own_state = jnp.einsum("si,ihef->shef", picker, state, precision=hi)
     own_ksum = jnp.einsum("si,ihe->she", picker, ksum, precision=hi)
     query_wide = query.astype(jnp.float32)

time: 176 us -> 220 us (1.25)
  waiting for transfers between devices: 62.4 us -> 110 us
  blocking collectives: 31.6 us -> 27.5 us
    psum x1 -> x2, waiting for transfers between devices: 30.4 us -> 79 us  [body(): state, ksum = lax.psum(lax.psum((state, ksum), 'rep'), 'seq')]
    psum x1 -> x2, blocking collectives: 31.6 us -> 27.5 us  [body(): state, ksum = lax.psum(lax.psum((state, ksum), 'rep'), 'seq')]
  transfers between devices with their start and end apart: 4 -> 5, of which waited for: 4 -> 5; matrix products, arithmetic and copies ran while one was open for 19% -> 16% of each run, Pallas kernels for 0% -> 0%
where the time goes in v1:
time: 220 us; the launch traced here: 219 us
  waiting for transfers between devices  110 us (50%)
  local copies, waits for them, and re-layouts  37.2 us (17%)
  blocking collectives  27.5 us (12%)
  matrix products  24.9 us (11%)
  between operations  13.4 us (6%)
  other arithmetic  5.39 us (2%)
    psum x2, waiting for transfers between devices, body(): state, ksum = lax.psum(lax.psum((state, ksum), 'rep'), 'seq')  79 us
    psum x2, blocking collectives, body(): state, ksum = lax.psum(lax.psum((state, ksum), 'rep'), 'seq')  27.5 us
    all_gather x1, waiting for transfers between devices, body(): lax.all_gather(attn, 'mp', axis=1, tiled=True)  26.8 us
    dot_general x2, local copies, waits for them, and re-layouts, body(): jnp.einsum('td,dcm->tcm', modulated, lax.all_gather(w_qkv, 'rep', axis=0,...  19.3 us
    dot_general x1, matrix products, body(): jnp.einsum('td,dcm->tcm', modulated, lax.all_gather(w_qkv, 'rep', axis=0,...  8.94 us
    unnamed x16, local copies, waits for them, and re-layouts  7.36 us
    dot_general x1, matrix products, body(): jnp.dot(lax.all_gather(attn, 'mp', axis=1, tiled=True), out_full, preferr...  5.59 us
  transfers between devices with their start and end apart: 5, of which 5 were waited for; matrix products, arithmetic and copies ran while one was open for 16% of the time, Pallas kernels for 0%

profile of v1, /device:TPU:0, one launch (start us, length us, event | category | flops | bytes accessed | tf_op | source)
XLA Modules:
  0.0 218.8 jit_solution(13188291324480106019)
XLA Ops:
  6.5 0.0 copy-start.1
  6.5 0.0 all-gather.4.cloned.1.call-start
  6.5 0.0 copy-start.3
  6.5 0.7 all-gather.4.cloned.1.call-update
  7.3 0.0 all-reduce.3.cloned.1.call-start
  7.3 0.2 copy-done.1
  7.5 0.2 reshape.54
  7.7 0.1 dot_general.41
  7.8 0.0 copy-done.3
  7.8 0.3 fusion.24
  8.1 0.4 copy.12
  8.5 2.7 %mul.34 = f32[2,256,2240]{1,0,2:T(2,128)S(1)} broadcast(f32[2,2240]{0,1:T(8,128)S(1)} %copy.12), dimensions={0,2} | broadcast | bytes 4605440 | tf_op jit(solution)/shard_map/mul | solution.py:26
  11.3 2.6 %copy.34 = f32[280,8,2,256]{3,1,2,0:T(8,128)} copy(f32[280,8,2,256]{3,2,1,0:T(2,128)S(1)} %bitcast.80) | data formatting | bytes 9175040
  13.8 0.4 copy.13
  14.2 0.0 slice-start
  14.2 2.7 %add.61 = f32[2,256,2240]{1,0,2:T(2,128)S(1)} broadcast(f32[2,2240]{0,1:T(8,128)S(1)} %copy.13), dimensions={0,2} | broadcast | bytes 4605440 | tf_op jit(solution)/shard_map/add | solution.py:26
  17.0 0.0 copy-start
  17.0 0.0 slice-start.1
  17.0 0.5 copy.35
  17.5 1.5 copy-done
  19.0 0.4 convert_reduce_fusion
  19.4 0.7 fusion.2
  20.1 0.0 slice-done
  20.1 0.0 slice-done.1
  20.1 3.0 %fusion.5 = bf16[512,2240]{0,1:T(8,128)(2,1)} fusion(f32[512,2240]{0,1:T(8,128)S(1)} %bitcast.79, f32[512,2240]{0,1:T(8,128)S(1)} %bitcast.78, bf16[512,2240]{0,1:T(8,128)(2,1)S(1)} %copy-done, f32[512]{0:T(512)S(1)} %add_sqrt_fusion, f32[512]{0:T(512)S(1)} %broadcast_multiply_fusion), kind=kLoop, calls=%fused_computation.7 | loop fusion | flops 6881280 | bytes 13766656 | tf_op jit(solution)/shard_map/convert_element_type | solution.py:26
  23.1 6.1 %dot_general.43 = bf16[2,256,2240]{1,0,2:T(2,128)(2,1)} reshape(bf16[512,2240]{0,1:T(8,128)(2,1)} %fusion.5) | data formatting | bytes 4587520 | tf_op jit(solution)/shard_map/td,dcm->tcm/dot_general | solution.py:30
  29.1 1.7 all-gather.4.cloned.1.call-done
  30.9 13.2 %copy.14 = bf16[3,640,2240]{2,1,0:T(8,128)(2,1)} copy(bf16[3,640,2240]{1,2,0:T(8,128)(2,1)} %bitcast.84) | data formatting | bytes 17203200 | tf_op jit(solution)/shard_map/td,dcm->tcm/dot_general | solution.py:30
  44.1 8.9 %fusion.10 = bf16[2,256,3,20,32]{1,4,3,2,0:T(8,128)(2,1)S(1)} fusion(bf16[3,20,32,2240,1]{3,2,1,0,4:T(8,128)(2,1)} %bitcast.83, bf16[2,256,2240,1,1]{1,0,2,4,3:T(2,128)(2,1)} %bitcast.88), kind=kOutput, calls=%fused_computation.13 | convolution fusion | flops 4404019200 | bytes 12861440 | tf_op jit(solution)/shard_map/td,dcm->tcm/dot_general | solution.py:30
  53.1 0.0 copy-start.2
  53.1 0.3 fusion.18
  53.4 1.9 fusion.22
  55.3 0.0 copy-done.2
  55.4 1.7 copy.20
  57.0 0.0 all-reduce.3.cloned.1.call-update
  57.0 0.0 all-reduce.5.cloned.1.call-start
  57.1 22.3 %all-reduce.3.cloned.1.call-done = f32[6,20,32,32]{3,2,1,0:T(8,128)} async-done(((f32[6,20,32,32]{3,2,1,0:T(8,128)}), f32[6,20,32,32]{3,2,1,0:T(8,128)}) %all-reduce.3.cloned.1.call-update) | async-done | bytes 491536 | tf_op jit(solution)/shard_map/psum | solution.py:44
  79.4 0.0 all-reduce.5.cloned.1.call-update
  79.5 0.0 all-gather.8.cloned.1.call-start
  79.5 0.5 all-gather.8.cloned.1.call-update
  80.0 0.0 all-gather.6.cloned.1.call-start
  80.1 1.3 convert_reduce_fusion.1
  81.4 0.3 fusion.33
  81.7 3.5 %psum.30 = f32[6,20,32]{2,1,0:T(8,128)S(1)} all-reduce(f32[6,20,32]{2,1,0:T(8,128)S(1)} %copy.24), channel_id=1, replica_groups=mesh['groups'=2,'seq'=4,'mp'=2,'rep'=2] {'rep'}, use_global_device_ids=true, to_apply=%region_5.6 | all-reduce | flops 3840 | bytes 30720 | tf_op jit(solution)/shard_map/psum | solution.py:44
  85.3 24.0 %psum.31 = f32[6,20,32]{2,1,0:T(8,128)S(1)} all-reduce(f32[6,20,32]{2,1,0:T(8,128)S(1)} %psum.30), channel_id=1, replica_groups=mesh['groups'=2,'seq'=4,'mp'=2,'rep'=2] {'seq'}, use_global_device_ids=true, to_apply=%region_6.7 | all-reduce | flops 3840 | bytes 30720 | tf_op jit(solution)/shard_map/psum | solution.py:44
  109.3 0.2 convolution_bitcast_fusion.1
  109.5 1.5 fusion.27
  111.0 56.7 %all-reduce.5.cloned.1.call-done = f32[6,20,32,32]{3,2,1,0:T(8,128)} async-done(((f32[6,20,32,32]{3,2,1,0:T(8,128)}), f32[6,20,32,32]{3,2,1,0:T(8,128)}) %all-reduce.5.cloned.1.call-update) | async-done | bytes 491536 | tf_op jit(solution)/shard_map/psum | solution.py:44
  167.7 3.9 %fusion.8 = f32[2,20,32,32]{3,0,2,1:T(2,128)S(1)} fusion(f32[6,20,32,32]{3,2,1,0:T(8,128)} %all-reduce.5.cloned.1.call-done, s32[2]{0:T(128)S(1)} %copy-done.3), kind=kOutput, calls=%fused_computation.11 | convolution fusion | flops 2949132 | bytes 655368 | tf_op jit(solution)/shard_map/si,ihef->shef/dot_general | solution.py:45
  171.7 1.9 fusion.13
  173.5 0.7 copy.16
  174.2 0.9 copy.36
  175.2 0.0 all-gather.6.cloned.1.call-update
  175.2 0.1 dynamic-slice_bitcast_fusion
  175.3 0.2 copy.11
  175.5 1.3 mul.31
  176.9 1.6 copy.33
  178.5 1.4 all-gather.8.cloned.1.call-done
  179.9 26.8 %all-gather.6.cloned.1.call-done = bf16[512,1280]{0,1:T(8,128)(2,1)} async-done(((bf16[512,640]{0,1:T(8,128)(2,1)}), bf16[512,1280]{0,1:T(8,128)(2,1)}) %all-gather.6.cloned.1.call-update) | async-done | bytes 1310736 | tf_op jit(solution)/shard_map/all_gather | solution.py:54
  206.7 5.6 %fusion.7 = bf16[512,1120]{0,1:T(8,128)(2,1)} fusion(f32[512,1120]{0,1:T(8,128)} %bitcast.87, bf16[1280,1120]{0,1:T(8,128)(2,1)} %all-gather.8.cloned.1.call-done, bf16[512,1280]{0,1:T(8,128)(2,1)} %all-gather.6.cloned.1.call-done, bf16[512,2240]{0,1:T(8,128)(2,1)S(1)} %copy-done, s32[]{:T(128)S(6)} %select_n.4), kind=kOutput, calls=%fused_computation.10 | convolution fusion | flops 1470300160 | bytes 8765444 | tf_op jit(solution)/shard_map/dot_general | solution.py:53
  (6 shorter events, 0.1 us)
Async XLA Ops:
  6.5 0.9 copy-start.1
  6.5 24.4 %all-gather.4.cloned.1.call-start = ((), (), s32[]{:S(2)}) async-start(), calls=%async_computation | async-start | bytes 12902400 | tf_op jit(solution)/shard_map/all_gather | solution.py:33
  6.5 1.3 copy-start.3
  7.3 72.2 %all-reduce.3.cloned.1.call-start = ((), (), s32[]{:S(2)}) async-start(), calls=%async_computation.1 | async-start | bytes 3932160 | tf_op jit(solution)/shard_map/psum | solution.py:44
  14.2 5.9 %slice-start = ((s8[4587520]{0:T(1024)(128)(4,1)}), s8[4194304]{0:T(1024)(128)(4,1)S(1)}, s32[]{:S(2)}) async-start(s8[4587520]{0:T(1024)(128)(4,1)} %bitcast.76), calls=%async_computation.5 | async-start | bytes 8388608
  17.0 2.1 copy-start
  17.0 3.1 %slice-start.1 = ((s8[4587520]{0:T(1024)(128)(4,1)}), s8[393216]{0:T(1024)(128)(4,1)S(1)}, s32[]{:S(2)}) async-start(s8[4587520]{0:T(1024)(128)(4,1)} %bitcast.76), calls=%async_computation.6 | async-start | bytes 786432
  53.1 2.3 %copy-start.2 = (bf16[2,256,3,20,32]{1,4,3,2,0:T(8,128)(2,1)}, bf16[2,256,3,20,32]{1,4,3,2,0:T(8,128)(2,1)S(1)}, u32[]{:S(2)}) copy-start(bf16[2,256,3,20,32]{1,4,3,2,0:T(8,128)(2,1)S(1)} %fusion.10) | copy-start | bytes 5898244
  57.0 110.7 %all-reduce.5.cloned.1.call-start = ((), (), s32[]{:S(2)}) async-start(), calls=%async_computation.2 | async-start | bytes 3932160 | tf_op jit(solution)/shard_map/psum | solution.py:44
  79.5 100.4 %all-gather.8.cloned.1.call-start = ((), (), s32[]{:S(2)}) async-start(), calls=%async_computation.4 | async-start | bytes 4300800 | tf_op jit(solution)/shard_map/all_gather | solution.py:51
  80.0 126.7 %all-gather.6.cloned.1.call-start = ((), (), s32[]{:S(2)}) async-start(), calls=%async_computation.3 | async-start | bytes 1966080 | tf_op jit(solution)/shard_map/all_gather | solution.py:54
Sparse Core Ops, SparseCore 0:
  8.9 21.9 all-gather.3
  57.2 22.2 all-reduce.2
  81.8 85.8 all-reduce.4
  169.1 10.6 all-gather.7
  181.3 25.3 all-gather.5
